TPU v7x, 512 devices: a whole 4x8x8 slice. The times are simulated.
512 devices in a mesh: lat: 16 (over x_hi, y), lon: 32 (over z, x_lo, core).
Axes of the slice: x: 4 (x_hi: 2, x_lo: 2; x = x_hi * 2 + x_lo), y: 8, z: 8, core: 2. Of those that a mesh axis runs over, the one named last changes fastest.
Arguments:
- height: float32 [1024, 8640], P('lat', 'lon'), may hold values from -6 to 6
- east_flow: float32 [1024, 8640], P('lat', 'lon'), may hold values from -4 to 4
- north_flow: float32 [1024, 8640], P('lat', 'lon'), may hold values from -4 to 4
- legendre: float32 [128, 1024, 2048], P('lon', 'lat'), may hold values from -0.1875 to 0.1875
- love_numbers: float32 [2048], replicated, may hold values from 0.05 to 1
- wavenumbers: int32 [128], replicated, may hold values from 0 to 2047, as said below
- land_sea: int32 [1024, 8640], P('lat', 'lon'), may hold values 0 or 1
Outputs:
- loading: float32 [1024, 8640], P('lat', 'lon')
- surface: float32 [1024, 8640], P('lat', 'lon')
- east_out: float32 [1024, 8640], P('lat', 'lon')
- north_out: float32 [1024, 8640], P('lat', 'lon')
Inputs may be any that keep to these rules, and one draw needn't show every extreme that they name: 128 distinct wavenumbers in no particular order; 0 and 2047 are always among them.
All inputs are finite; a program needn't handle non-finite values. No bound on the sum of `land_sea` on one device may be relied on, other than what follows from the above.
Results may differ from a plain program's by a relative error of at most 0.000078.
Values sent between devices are 32-bit elements; how exact they have to be, the bound alone decides.
A program may use at most 64 MiB of HBM per device.

v0:
```python
import math
import jax
import jax.numpy as jnp
from jax import lax
from jax.sharding import PartitionSpec as P

SUBSTEPS = 4
east_step = 0.3
north_step = 0.3


def extended(block, sides, width, periodic):
    for axis, dim in sides:
        count = lax.axis_size(axis)
        forward = [(i, i + 1) for i in range(count - 1)]
        if periodic:
            forward.append((count - 1, 0))
        backward = [(target, source) for source, target in forward]
        low = lax.ppermute(
            lax.slice_in_dim(block, block.shape[dim] - width, None, axis=dim), axis, forward
        )
        high = lax.ppermute(lax.slice_in_dim(block, 0, width, axis=dim), axis, backward)
        block = jnp.concatenate([low, block, high], axis=dim)
    return block


def harmonic_rows(wavenumbers, first_column, column_count, period):
    columns = first_column + jnp.arange(column_count, dtype=jnp.int32)
    product = wavenumbers[:, None] * columns[None, :] % period
    angles = 2.0 * math.pi / period * product.astype(jnp.float32)
    stacked = jnp.stack([jnp.cos(angles), jnp.sin(angles)], axis=1)
    return stacked.reshape(2 * wavenumbers.shape[0], column_count)


def band_rim(field):
    return extended(field, (("lat", 0),), 1, False)


def sector_rim(field):
    return extended(field, (("lon", 1),), 1, True)


def shards(height, east_flow, north_flow, legendre, love_numbers, wavenumbers, land_sea):
    highest = lax.Precision.HIGHEST
    band_rows, sector_cols = height.shape
    all_cols = sector_cols * lax.axis_size("lon")
    all_waves = wavenumbers.shape[0]
    own_waves = legendre.shape[0]
    sector_index = lax.axis_index("lon")
    harmonics = harmonic_rows(wavenumbers, sector_index * sector_cols, sector_cols, all_cols)
    forward_scale = 1.0 / math.sqrt(all_cols)
    partial_rows = forward_scale * lax.dot_general(
        harmonics, height, (((1,), (1,)), ((), ())), precision=highest
    )
    totals = lax.psum(partial_rows, "lon")
    owned = lax.dynamic_slice_in_dim(totals, sector_index * (2 * own_waves), 2 * own_waves, 0)
    owned = owned.reshape(own_waves, 2, band_rows)
    partial_value = jnp.einsum("mtl,mpt->mpl", legendre, owned, precision=highest)
    spectral = lax.psum(partial_value, "lat") * love_numbers[None, None, :]
    synthesized = jnp.einsum("mtl,mpl->mpt", legendre, spectral, precision=highest).reshape(
        2 * own_waves, band_rows
    )
    back_scale = 1.0 / math.sqrt(all_waves)
    loading = (
        lax.dot_general(
            lax.all_gather(synthesized, "lon", axis=0, tiled=True),
            harmonics,
            (((0,), (0,)), ((), ())),
            precision=highest,
        )
        * back_scale
    )
    wet_cells = land_sea.astype(jnp.float32)
    surface = height
    east_out = east_flow
    north_out = north_flow
    for substep in range(SUBSTEPS):
        pressure = surface - loading
        pressure_lat = band_rim(pressure)
        pressure_lon = sector_rim(pressure)
        east_out = wet_cells * (east_out - east_step * (pressure_lon[:, 2:] - pressure_lon[:, :-2]))
        north_out = wet_cells * (north_out - north_step * (pressure_lat[2:] - pressure_lat[:-2]))
        east_wide = sector_rim(east_out)
        north_wide = band_rim(north_out)
        change = east_step * (east_wide[:, 2:] - east_wide[:, :-2]) + north_step * (
            north_wide[2:] - north_wide[:-2]
        )
        surface = surface - wet_cells * change
    return (loading, surface, east_out, north_out)


def solution(mesh):
    return jax.shard_map(
        shards,
        mesh=mesh,
        in_specs=(
            P("lat", "lon"),
            P("lat", "lon"),
            P("lat", "lon"),
            P("lon", "lat", None),
            P(),
            P(),
            P("lat", "lon"),
        ),
        out_specs=(P("lat", "lon"), P("lat", "lon"), P("lat", "lon"), P("lat", "lon")),
        check_vma=False,
    )
```

profile of v0, /device:TPU:56, one launch (start us, length us, event | category | flops | bytes accessed | tf_op | source)
XLA Modules:
  0.0 582.8 jit_solution(6953861917037026702)
XLA Ops:
  7.2 7.9 %fusion.62 = (f32[128,1,270]{2,1,0:T(1,128)S(1)}, f32[128,1,270]{2,1,0:T(1,128)S(1)}) fusion(s32[270]{0:T(512)S(1)} %iota_add_fusion, s32[128]{0:T(128)} %param.12), kind=kLoop, calls=%fused_computation.98 | loop fusion | flops 311040 | bytes 278072 | tf_op jit(solution)/shard_map/cos | solution.py:31
  15.9 2.0 convolution_multiply_fusion
  18.0 215.3 %all-reduce.3.cloned.1.call-done = f32[256,64]{1,0:T(8,128)} async-done(((f32[256,64]{1,0:T(8,128)}), f32[256,64]{1,0:T(8,128)}) %all-reduce.3.cloned.1.call-update) | async-done | bytes 65552 | tf_op jit(solution)/shard_map/psum | solution.py:55
  233.9 1.7 fusion.86
  235.7 149.2 %all-reduce.5.cloned.1.call-done = f32[4,2,2048]{2,1,0:T(2,128)} async-done(((f32[4,2,2048]{2,1,0:T(2,128)}), f32[4,2,2048]{2,1,0:T(2,128)}) %all-reduce.5.cloned.1.call-update) | async-done | bytes 65552 | tf_op jit(solution)/shard_map/psum | solution.py:59
  384.8 2.7 fusion.58
  387.5 35.5 %all_gather.3 = f32[256,64]{1,0:T(8,128)S(1)} all-gather(f32[8,64]{1,0:T(8,128)S(1)} %bitcast.9), channel_id=1, replica_groups=mesh['lat'=16,'lon'=32] {'lon'}, dimensions={0}, use_global_device_ids=true | all-gather | bytes 67584 | tf_op jit(solution)/shard_map/all_gather | solution.py:66
  423.5 1.9 collective-permute-start.4
  425.4 7.5 %collective-permute-start.5 = (f32[1,270]{1,0:T(1,128)S(1)}, f32[1,270]{1,0:T(1,128)S(1)}, u32[]{:S(2)}, u32[]{:S(2)}) collective-permute-start(f32[1,270]{1,0:T(1,128)S(1)} %get-tuple-element.49), channel_id=1, source_target_pairs={{0,32},{32,64},{64,96},{96,128},{128,160},{160,192},{192,224},{224... | collective-permute-start | bytes 3248 | tf_op jit(solution)/shard_map/ppermute | solution.py:19
  433.0 1.9 collective-permute-start
  435.0 2.4 collective-permute-start.1
  437.4 4.9 collective-permute-done.1
  442.5 1.9 collective-permute-start.6
  444.4 7.5 %collective-permute-start.7 = (f32[1,270]{1,0:T(1,128)S(1)}, f32[1,270]{1,0:T(1,128)S(1)}, u32[]{:S(2)}, u32[]{:S(2)}) collective-permute-start(f32[1,270]{1,0:T(1,128)S(1)} %get-tuple-element.47), channel_id=1, source_target_pairs={{0,32},{32,64},{64,96},{96,128},{128,160},{160,192},{192,224},{224... | collective-permute-start | bytes 3248 | tf_op jit(solution)/shard_map/ppermute | solution.py:19
  452.0 1.9 collective-permute-start.2
  454.0 2.4 collective-permute-start.3
  456.4 4.9 collective-permute-done.3
  461.5 1.9 collective-permute-start.12
  463.4 7.5 %collective-permute-start.13 = (f32[1,270]{1,0:T(1,128)S(1)}, f32[1,270]{1,0:T(1,128)S(1)}, u32[]{:S(2)}, u32[]{:S(2)}) collective-permute-start(f32[1,270]{1,0:T(1,128)S(1)} %get-tuple-element.41), channel_id=1, source_target_pairs={{0,32},{32,64},{64,96},{96,128},{128,160},{160,192},{192,224},{224... | collective-permute-start | bytes 3248 | tf_op jit(solution)/shard_map/ppermute | solution.py:19
  471.0 1.9 collective-permute-start.8
  472.9 2.4 collective-permute-start.9
  475.4 4.9 collective-permute-done.9
  480.4 1.9 collective-permute-start.14
  482.4 7.5 %collective-permute-start.15 = (f32[1,270]{1,0:T(1,128)S(1)}, f32[1,270]{1,0:T(1,128)S(1)}, u32[]{:S(2)}, u32[]{:S(2)}) collective-permute-start(f32[1,270]{1,0:T(1,128)S(1)} %get-tuple-element.39), channel_id=1, source_target_pairs={{0,32},{32,64},{64,96},{96,128},{128,160},{160,192},{192,224},{224... | collective-permute-start | bytes 3248 | tf_op jit(solution)/shard_map/ppermute | solution.py:19
  490.0 1.9 collective-permute-start.10
  491.9 2.4 collective-permute-start.11
  494.3 4.9 collective-permute-done.11
  499.4 1.9 collective-permute-start.20
  501.3 7.5 %collective-permute-start.21 = (f32[1,270]{1,0:T(1,128)S(1)}, f32[1,270]{1,0:T(1,128)S(1)}, u32[]{:S(2)}, u32[]{:S(2)}) collective-permute-start(f32[1,270]{1,0:T(1,128)S(1)} %get-tuple-element.33), channel_id=1, source_target_pairs={{0,32},{32,64},{64,96},{96,128},{128,160},{160,192},{192,224},{224... | collective-permute-start | bytes 3248 | tf_op jit(solution)/shard_map/ppermute | solution.py:19
  509.0 1.9 collective-permute-start.16
  510.9 2.4 collective-permute-start.17
  513.3 4.9 collective-permute-done.17
  518.4 1.9 collective-permute-start.22
  520.3 7.5 %collective-permute-start.23 = (f32[1,270]{1,0:T(1,128)S(1)}, f32[1,270]{1,0:T(1,128)S(1)}, u32[]{:S(2)}, u32[]{:S(2)}) collective-permute-start(f32[1,270]{1,0:T(1,128)S(1)} %get-tuple-element.31), channel_id=1, source_target_pairs={{0,32},{32,64},{64,96},{96,128},{128,160},{160,192},{192,224},{224... | collective-permute-start | bytes 3248 | tf_op jit(solution)/shard_map/ppermute | solution.py:19
  527.9 1.9 collective-permute-start.18
  529.9 2.4 collective-permute-start.19
  532.3 4.9 collective-permute-done.19
  537.4 1.9 collective-permute-start.28
  539.3 7.5 %collective-permute-start.29 = (f32[1,270]{1,0:T(1,128)S(1)}, f32[1,270]{1,0:T(1,128)S(1)}, u32[]{:S(2)}, u32[]{:S(2)}) collective-permute-start(f32[1,270]{1,0:T(1,128)S(1)} %get-tuple-element.25), channel_id=1, source_target_pairs={{0,32},{32,64},{64,96},{96,128},{128,160},{160,192},{192,224},{224... | collective-permute-start | bytes 3248 | tf_op jit(solution)/shard_map/ppermute | solution.py:19
  546.9 1.9 collective-permute-start.24
  548.8 2.4 collective-permute-start.25
  551.3 4.9 collective-permute-done.25
  556.4 1.9 collective-permute-start.30
  558.3 7.5 %collective-permute-start.31 = (f32[1,270]{1,0:T(1,128)S(1)}, f32[1,270]{1,0:T(1,128)S(1)}, u32[]{:S(2)}, u32[]{:S(2)}) collective-permute-start(f32[1,270]{1,0:T(1,128)S(1)} %get-tuple-element.23), channel_id=1, source_target_pairs={{0,32},{32,64},{64,96},{96,128},{128,160},{160,192},{192,224},{224... | collective-permute-start | bytes 3248 | tf_op jit(solution)/shard_map/ppermute | solution.py:19
  565.9 1.9 collective-permute-start.26
  567.8 2.4 collective-permute-start.27
  570.3 4.9 collective-permute-done.27
  575.2 0.8 fusion.6
  (74 shorter events, 3.6 us)
Async XLA Ops:
  7.2 226.8 %copy-start = (f32[4,64,2048]{2,1,0:T(8,128)S(1)}, f32[4,64,2048]{2,1,0:T(8,128)}, u32[]{:S(2)}) copy-start(f32[4,64,2048]{2,1,0:T(8,128)} %param.10) | copy-start | bytes 6291460
  7.2 226.1 %all-reduce.3.cloned.1.call-start = ((), (), s32[]{:S(2)}) async-start(), calls=%async_computation | async-start | bytes 262144 | tf_op jit(solution)/shard_map/psum | solution.py:55
  15.2 369.7 %copy-start.8 = (f32[2048]{0:T(1024)S(1)}, f32[2048]{0:T(1024)}, u32[]{:S(2)}) copy-start(f32[2048]{0:T(1024)} %param.11) | copy-start | bytes 24580
  17.9 366.9 %all-reduce.5.cloned.1.call-start = ((), (), s32[]{:S(2)}) async-start(), calls=%async_computation.1 | async-start | bytes 131072 | tf_op jit(solution)/shard_map/psum | solution.py:59
  233.9 189.1 %copy-start.3 = (f32[64,270]{1,0:T(8,128)S(1)}, f32[64,270]{1,0:T(8,128)}, u32[]{:S(2)}) copy-start(f32[64,270]{1,0:T(8,128)} %param.7) | copy-start | bytes 207364
  235.7 206.7 %copy-start.1 = (s32[64,270]{1,0:T(8,128)S(1)}, s32[64,270]{1,0:T(8,128)}, u32[]{:S(2)}) copy-start(s32[64,270]{1,0:T(8,128)} %param.13) | copy-start | bytes 207364
  235.7 206.7 %copy-start.6 = (f32[64,270]{1,0:T(8,128)S(1)}, f32[64,270]{1,0:T(8,128)}, u32[]{:S(2)}) copy-start(f32[64,270]{1,0:T(8,128)} %param.8) | copy-start | bytes 207364
  235.7 206.7 %copy-start.7 = (f32[64,270]{1,0:T(8,128)S(1)}, f32[64,270]{1,0:T(8,128)}, u32[]{:S(2)}) copy-start(f32[64,270]{1,0:T(8,128)} %param.9) | copy-start | bytes 207364
  423.5 113.7 %copy-start.2 = (f32[64,270]{1,0:T(8,128)}, f32[64,270]{1,0:T(8,128)S(1)}, u32[]{:S(2)}) copy-start(f32[64,270]{1,0:T(8,128)S(1)} %get-tuple-element.53) | copy-start | bytes 207364
  423.5 18.8 %collective-permute-start.4 = (f32[1,270]{1,0:T(1,128)S(1)}, f32[1,270]{1,0:T(1,128)S(1)}, u32[]{:S(2)}, u32[]{:S(2)}) collective-permute-start(f32[1,270]{1,0:T(1,128)S(1)} %get-tuple-element.48), channel_id=1, source_target_pairs={{32,0},{64,32},{96,64},{128,96},{160,128},{192,160},{224,192},{256... | collective-permute-start | bytes 3248 | tf_op jit(solution)/shard_map/ppermute | solution.py:22
  425.4 16.9 %collective-permute-start.5 = (f32[1,270]{1,0:T(1,128)S(1)}, f32[1,270]{1,0:T(1,128)S(1)}, u32[]{:S(2)}, u32[]{:S(2)}) collective-permute-start(f32[1,270]{1,0:T(1,128)S(1)} %get-tuple-element.49), channel_id=1, source_target_pairs={{0,32},{32,64},{64,96},{96,128},{128,160},{160,192},{192,224},{224... | collective-permute-start | bytes 3248 | tf_op jit(solution)/shard_map/ppermute | solution.py:19
  433.0 4.3 collective-permute-start
  435.0 7.3 %collective-permute-start.1 = (f32[64,1]{1,0:T(8,128)S(1)}, f32[64,1]{1,0:T(8,128)S(1)}, u32[]{:S(2)}, u32[]{:S(2)}) collective-permute-start(f32[64,1]{1,0:T(8,128)S(1)} %get-tuple-element.45), channel_id=1, source_target_pairs={{0,1},{1,2},{2,3},{3,4},{4,5},{5,6},{6,7},{7,8},{8,9},{9,10},{10,1... | collective-permute-start | bytes 776 | tf_op jit(solution)/shard_map/ppermute | solution.py:19
  442.5 18.8 %collective-permute-start.6 = (f32[1,270]{1,0:T(1,128)S(1)}, f32[1,270]{1,0:T(1,128)S(1)}, u32[]{:S(2)}, u32[]{:S(2)}) collective-permute-start(f32[1,270]{1,0:T(1,128)S(1)} %get-tuple-element.46), channel_id=1, source_target_pairs={{32,0},{64,32},{96,64},{128,96},{160,128},{192,160},{224,192},{256... | collective-permute-start | bytes 3248 | tf_op jit(solution)/shard_map/ppermute | solution.py:22
  444.4 16.9 %collective-permute-start.7 = (f32[1,270]{1,0:T(1,128)S(1)}, f32[1,270]{1,0:T(1,128)S(1)}, u32[]{:S(2)}, u32[]{:S(2)}) collective-permute-start(f32[1,270]{1,0:T(1,128)S(1)} %get-tuple-element.47), channel_id=1, source_target_pairs={{0,32},{32,64},{64,96},{96,128},{128,160},{160,192},{192,224},{224... | collective-permute-start | bytes 3248 | tf_op jit(solution)/shard_map/ppermute | solution.py:19
  452.0 4.3 collective-permute-start.2
  454.0 7.3 %collective-permute-start.3 = (f32[64,1]{1,0:T(8,128)S(1)}, f32[64,1]{1,0:T(8,128)S(1)}, u32[]{:S(2)}, u32[]{:S(2)}) collective-permute-start(f32[64,1]{1,0:T(8,128)S(1)} %get-tuple-element.43), channel_id=1, source_target_pairs={{0,1},{1,2},{2,3},{3,4},{4,5},{5,6},{6,7},{7,8},{8,9},{9,10},{10,1... | collective-permute-start | bytes 776 | tf_op jit(solution)/shard_map/ppermute | solution.py:19
  461.5 18.8 %collective-permute-start.12 = (f32[1,270]{1,0:T(1,128)S(1)}, f32[1,270]{1,0:T(1,128)S(1)}, u32[]{:S(2)}, u32[]{:S(2)}) collective-permute-start(f32[1,270]{1,0:T(1,128)S(1)} %get-tuple-element.40), channel_id=1, source_target_pairs={{32,0},{64,32},{96,64},{128,96},{160,128},{192,160},{224,192},{256... | collective-permute-start | bytes 3248 | tf_op jit(solution)/shard_map/ppermute | solution.py:22
  463.4 16.9 %collective-permute-start.13 = (f32[1,270]{1,0:T(1,128)S(1)}, f32[1,270]{1,0:T(1,128)S(1)}, u32[]{:S(2)}, u32[]{:S(2)}) collective-permute-start(f32[1,270]{1,0:T(1,128)S(1)} %get-tuple-element.41), channel_id=1, source_target_pairs={{0,32},{32,64},{64,96},{96,128},{128,160},{160,192},{192,224},{224... | collective-permute-start | bytes 3248 | tf_op jit(solution)/shard_map/ppermute | solution.py:19
  471.0 4.3 collective-permute-start.8
  472.9 7.3 %collective-permute-start.9 = (f32[64,1]{1,0:T(8,128)S(1)}, f32[64,1]{1,0:T(8,128)S(1)}, u32[]{:S(2)}, u32[]{:S(2)}) collective-permute-start(f32[64,1]{1,0:T(8,128)S(1)} %get-tuple-element.37), channel_id=1, source_target_pairs={{0,1},{1,2},{2,3},{3,4},{4,5},{5,6},{6,7},{7,8},{8,9},{9,10},{10,1... | collective-permute-start | bytes 776 | tf_op jit(solution)/shard_map/ppermute | solution.py:19
  480.4 18.8 %collective-permute-start.14 = (f32[1,270]{1,0:T(1,128)S(1)}, f32[1,270]{1,0:T(1,128)S(1)}, u32[]{:S(2)}, u32[]{:S(2)}) collective-permute-start(f32[1,270]{1,0:T(1,128)S(1)} %get-tuple-element.38), channel_id=1, source_target_pairs={{32,0},{64,32},{96,64},{128,96},{160,128},{192,160},{224,192},{256... | collective-permute-start | bytes 3248 | tf_op jit(solution)/shard_map/ppermute | solution.py:22
  482.4 16.9 %collective-permute-start.15 = (f32[1,270]{1,0:T(1,128)S(1)}, f32[1,270]{1,0:T(1,128)S(1)}, u32[]{:S(2)}, u32[]{:S(2)}) collective-permute-start(f32[1,270]{1,0:T(1,128)S(1)} %get-tuple-element.39), channel_id=1, source_target_pairs={{0,32},{32,64},{64,96},{96,128},{128,160},{160,192},{192,224},{224... | collective-permute-start | bytes 3248 | tf_op jit(solution)/shard_map/ppermute | solution.py:19
  490.0 4.3 collective-permute-start.10
  491.9 7.3 %collective-permute-start.11 = (f32[64,1]{1,0:T(8,128)S(1)}, f32[64,1]{1,0:T(8,128)S(1)}, u32[]{:S(2)}, u32[]{:S(2)}) collective-permute-start(f32[64,1]{1,0:T(8,128)S(1)} %get-tuple-element.35), channel_id=1, source_target_pairs={{0,1},{1,2},{2,3},{3,4},{4,5},{5,6},{6,7},{7,8},{8,9},{9,10},{10,1... | collective-permute-start | bytes 776 | tf_op jit(solution)/shard_map/ppermute | solution.py:19
  499.4 18.8 %collective-permute-start.20 = (f32[1,270]{1,0:T(1,128)S(1)}, f32[1,270]{1,0:T(1,128)S(1)}, u32[]{:S(2)}, u32[]{:S(2)}) collective-permute-start(f32[1,270]{1,0:T(1,128)S(1)} %get-tuple-element.32), channel_id=1, source_target_pairs={{32,0},{64,32},{96,64},{128,96},{160,128},{192,160},{224,192},{256... | collective-permute-start | bytes 3248 | tf_op jit(solution)/shard_map/ppermute | solution.py:22
  501.3 16.9 %collective-permute-start.21 = (f32[1,270]{1,0:T(1,128)S(1)}, f32[1,270]{1,0:T(1,128)S(1)}, u32[]{:S(2)}, u32[]{:S(2)}) collective-permute-start(f32[1,270]{1,0:T(1,128)S(1)} %get-tuple-element.33), channel_id=1, source_target_pairs={{0,32},{32,64},{64,96},{96,128},{128,160},{160,192},{192,224},{224... | collective-permute-start | bytes 3248 | tf_op jit(solution)/shard_map/ppermute | solution.py:19
  509.0 4.3 collective-permute-start.16
  510.9 7.3 %collective-permute-start.17 = (f32[64,1]{1,0:T(8,128)S(1)}, f32[64,1]{1,0:T(8,128)S(1)}, u32[]{:S(2)}, u32[]{:S(2)}) collective-permute-start(f32[64,1]{1,0:T(8,128)S(1)} %get-tuple-element.29), channel_id=1, source_target_pairs={{0,1},{1,2},{2,3},{3,4},{4,5},{5,6},{6,7},{7,8},{8,9},{9,10},{10,1... | collective-permute-start | bytes 776 | tf_op jit(solution)/shard_map/ppermute | solution.py:19
  518.4 18.8 %collective-permute-start.22 = (f32[1,270]{1,0:T(1,128)S(1)}, f32[1,270]{1,0:T(1,128)S(1)}, u32[]{:S(2)}, u32[]{:S(2)}) collective-permute-start(f32[1,270]{1,0:T(1,128)S(1)} %get-tuple-element.30), channel_id=1, source_target_pairs={{32,0},{64,32},{96,64},{128,96},{160,128},{192,160},{224,192},{256... | collective-permute-start | bytes 3248 | tf_op jit(solution)/shard_map/ppermute | solution.py:22
  520.3 16.9 %collective-permute-start.23 = (f32[1,270]{1,0:T(1,128)S(1)}, f32[1,270]{1,0:T(1,128)S(1)}, u32[]{:S(2)}, u32[]{:S(2)}) collective-permute-start(f32[1,270]{1,0:T(1,128)S(1)} %get-tuple-element.31), channel_id=1, source_target_pairs={{0,32},{32,64},{64,96},{96,128},{128,160},{160,192},{192,224},{224... | collective-permute-start | bytes 3248 | tf_op jit(solution)/shard_map/ppermute | solution.py:19
  527.9 4.3 collective-permute-start.18
  529.9 7.3 %collective-permute-start.19 = (f32[64,1]{1,0:T(8,128)S(1)}, f32[64,1]{1,0:T(8,128)S(1)}, u32[]{:S(2)}, u32[]{:S(2)}) collective-permute-start(f32[64,1]{1,0:T(8,128)S(1)} %get-tuple-element.27), channel_id=1, source_target_pairs={{0,1},{1,2},{2,3},{3,4},{4,5},{5,6},{6,7},{7,8},{8,9},{9,10},{10,1... | collective-permute-start | bytes 776 | tf_op jit(solution)/shard_map/ppermute | solution.py:19
  537.4 18.8 %collective-permute-start.28 = (f32[1,270]{1,0:T(1,128)S(1)}, f32[1,270]{1,0:T(1,128)S(1)}, u32[]{:S(2)}, u32[]{:S(2)}) collective-permute-start(f32[1,270]{1,0:T(1,128)S(1)} %get-tuple-element.24), channel_id=1, source_target_pairs={{32,0},{64,32},{96,64},{128,96},{160,128},{192,160},{224,192},{256... | collective-permute-start | bytes 3248 | tf_op jit(solution)/shard_map/ppermute | solution.py:22
  539.3 16.9 %collective-permute-start.29 = (f32[1,270]{1,0:T(1,128)S(1)}, f32[1,270]{1,0:T(1,128)S(1)}, u32[]{:S(2)}, u32[]{:S(2)}) collective-permute-start(f32[1,270]{1,0:T(1,128)S(1)} %get-tuple-element.25), channel_id=1, source_target_pairs={{0,32},{32,64},{64,96},{96,128},{128,160},{160,192},{192,224},{224... | collective-permute-start | bytes 3248 | tf_op jit(solution)/shard_map/ppermute | solution.py:19
  546.9 4.3 collective-permute-start.24
  548.8 7.3 %collective-permute-start.25 = (f32[64,1]{1,0:T(8,128)S(1)}, f32[64,1]{1,0:T(8,128)S(1)}, u32[]{:S(2)}, u32[]{:S(2)}) collective-permute-start(f32[64,1]{1,0:T(8,128)S(1)} %get-tuple-element.21), channel_id=1, source_target_pairs={{0,1},{1,2},{2,3},{3,4},{4,5},{5,6},{6,7},{7,8},{8,9},{9,10},{10,1... | collective-permute-start | bytes 776 | tf_op jit(solution)/shard_map/ppermute | solution.py:19
  556.3 19.6 %copy-start.4 = (f32[64,270]{1,0:T(8,128)}, f32[64,270]{1,0:T(8,128)S(1)}, u32[]{:S(2)}) copy-start(f32[64,270]{1,0:T(8,128)S(1)} %get-tuple-element.10) | copy-start | bytes 207364
  556.3 19.6 %copy-start.5 = (f32[64,270]{1,0:T(8,128)}, f32[64,270]{1,0:T(8,128)S(1)}, u32[]{:S(2)}) copy-start(f32[64,270]{1,0:T(8,128)S(1)} %get-tuple-element.11) | copy-start | bytes 207364
  556.4 18.8 %collective-permute-start.30 = (f32[1,270]{1,0:T(1,128)S(1)}, f32[1,270]{1,0:T(1,128)S(1)}, u32[]{:S(2)}, u32[]{:S(2)}) collective-permute-start(f32[1,270]{1,0:T(1,128)S(1)} %get-tuple-element.22), channel_id=1, source_target_pairs={{32,0},{64,32},{96,64},{128,96},{160,128},{192,160},{224,192},{256... | collective-permute-start | bytes 3248 | tf_op jit(solution)/shard_map/ppermute | solution.py:22
  558.3 16.9 %collective-permute-start.31 = (f32[1,270]{1,0:T(1,128)S(1)}, f32[1,270]{1,0:T(1,128)S(1)}, u32[]{:S(2)}, u32[]{:S(2)}) collective-permute-start(f32[1,270]{1,0:T(1,128)S(1)} %get-tuple-element.23), channel_id=1, source_target_pairs={{0,32},{32,64},{64,96},{96,128},{128,160},{160,192},{192,224},{224... | collective-permute-start | bytes 3248 | tf_op jit(solution)/shard_map/ppermute | solution.py:19
  565.9 4.3 collective-permute-start.26
  567.8 7.3 %collective-permute-start.27 = (f32[64,1]{1,0:T(8,128)S(1)}, f32[64,1]{1,0:T(8,128)S(1)}, u32[]{:S(2)}, u32[]{:S(2)}) collective-permute-start(f32[64,1]{1,0:T(8,128)S(1)} %get-tuple-element.19), channel_id=1, source_target_pairs={{0,1},{1,2},{2,3},{3,4},{4,5},{5,6},{6,7},{7,8},{8,9},{9,10},{10,1... | collective-permute-start | bytes 776 | tf_op jit(solution)/shard_map/ppermute | solution.py:19
Sparse Core Ops, SparseCore 0:
  18.0 215.1 all-reduce.2
  236.7 148.0 all-reduce.4
where the time goes:
time: 584 us; the launch traced here: 583 us
  waiting for transfers between devices  404 us (69%)
  starting transfers between devices  110 us (19%)
  blocking collectives  35.5 us (6%)
  between operations  14.6 us (2%)
  other arithmetic  10 us (2%)
  matrix products  6.82 us (1%)
    psum x1, waiting for transfers between devices, shards(): totals = lax.psum(partial_rows, 'lon')  215 us
    psum x1, waiting for transfers between devices, shards(): spectral = lax.psum(partial_value, 'lat') * love_numbers[None, None, :]  149 us
    ppermute x16, starting transfers between devices, extended(): lax.ppermute(lax.slice_in_dim(block, block.shape[dim] - width, None, axis...  79.5 us
    ppermute x16, waiting for transfers between devices, extended(): lax.ppermute(lax.slice_in_dim(block, block.shape[dim] - width, None, axis...  39.4 us
    all_gather x1, blocking collectives, shards(): lax.all_gather(synthesized, 'lon', axis=0, tiled=True)  35.5 us
    ppermute x16, starting transfers between devices, extended(): lax.ppermute(lax.slice_in_dim(block, 0, width, axis=dim), axis, backward)  30.7 us
  transfers between devices with their start and end apart: 34, of which 10 were waited for; matrix products, arithmetic and copies ran while one was open for 0% of the time, Pallas kernels for 0%

commit v1 on v0

--- a/solution.py
+++ b/solution.py
@@ -56,7 +56,7 @@
     owned = lax.dynamic_slice_in_dim(totals, sector_index * (2 * own_waves), 2 * own_waves, 0)
     owned = owned.reshape(own_waves, 2, band_rows)
     partial_value = jnp.einsum("mtl,mpt->mpl", legendre, owned, precision=highest)
-    spectral = lax.psum(partial_value, "lat") * love_numbers[None, None, :]
+    spectral = jnp.sum(lax.all_gather(partial_value, "lat"), axis=0) * love_numbers[None, None, :]
     synthesized = jnp.einsum("mtl,mpl->mpt", legendre, spectral, precision=highest).reshape(
         2 * own_waves, band_rows
     )

time: 584 us -> 519 us (0.89)
  waiting for transfers between devices: 404 us -> 338 us
    psum x1 -> x0, waiting for transfers between devices: 149 us -> none  [shards(): spectral = lax.psum(partial_value, 'lat') * love_numbers[None, None, :]]
    all_gather x0 -> x1, waiting for transfers between devices: none -> 83.5 us  [shards(): lax.all_gather(partial_value, 'lat')]
where the time goes in v1:
time: 519 us; the launch traced here: 517 us
  waiting for transfers between devices  338 us (65%)
  starting transfers between devices  110 us (21%)
  blocking collectives  34.6 us (7%)
  between operations  14.6 us (3%)
  other arithmetic  11.7 us (2%)
  matrix products  6 us (1%)
    psum x1, waiting for transfers between devices, shards(): totals = lax.psum(partial_rows, 'lon')  215 us
    all_gather x1, waiting for transfers between devices, shards(): lax.all_gather(partial_value, 'lat')  83.5 us
    ppermute x16, starting transfers between devices, extended(): lax.ppermute(lax.slice_in_dim(block, block.shape[dim] - width, None, axis...  78.1 us
    ppermute x16, waiting for transfers between devices, extended(): lax.ppermute(lax.slice_in_dim(block, block.shape[dim] - width, None, axis...  39.4 us
    all_gather x1, blocking collectives, shards(): lax.all_gather(synthesized, 'lon', axis=0, tiled=True)  34.6 us
    ppermute x16, starting transfers between devices, extended(): lax.ppermute(lax.slice_in_dim(block, 0, width, axis=dim), axis, backward)  32.1 us
  transfers between devices with their start and end apart: 34, of which 10 were waited for; matrix products, arithmetic and copies ran while one was open for 0% of the time, Pallas kernels for 0%

profile of v1, /device:TPU:56, one launch (start us, length us, event | category | flops | bytes accessed | tf_op | source)
XLA Modules:
  0.0 517.2 jit_solution(3907386236394708143)
XLA Ops:
  7.2 7.9 %fusion.62 = (f32[128,1,270]{2,1,0:T(1,128)S(1)}, f32[128,1,270]{2,1,0:T(1,128)S(1)}) fusion(s32[270]{0:T(512)S(1)} %iota_add_fusion, s32[128]{0:T(128)} %param.12), kind=kLoop, calls=%fused_computation.98 | loop fusion | flops 311040 | bytes 278072 | tf_op jit(solution)/shard_map/cos | solution.py:31
  15.9 2.0 convolution_multiply_fusion
  18.0 215.3 %all-reduce.2.cloned.1.call-done = f32[256,64]{1,0:T(8,128)} async-done(((f32[256,64]{1,0:T(8,128)}), f32[256,64]{1,0:T(8,128)}) %all-reduce.2.cloned.1.call-update) | async-done | bytes 65552 | tf_op jit(solution)/shard_map/psum | solution.py:55
  233.9 1.7 fusion.86
  235.7 83.5 %all-gather.3.cloned.1.call-done = f32[64,2,2048]{2,1,0:T(2,128)} async-done(((f32[4,2,2048]{2,1,0:T(2,128)}), f32[64,2,2048]{2,1,0:T(2,128)}) %all-gather.3.cloned.1.call-update) | async-done | bytes 1048592 | tf_op jit(solution)/shard_map/all_gather | solution.py:59
  319.2 1.7 reduce_sum.9
  320.9 1.8 fusion.58
  322.7 34.6 %all_gather.11 = f32[256,64]{1,0:T(8,128)S(1)} all-gather(f32[8,64]{1,0:T(8,128)S(1)} %bitcast.11), channel_id=1, replica_groups=mesh['lat'=16,'lon'=32] {'lon'}, dimensions={0}, use_global_device_ids=true | all-gather | bytes 67584 | tf_op jit(solution)/shard_map/all_gather | solution.py:66
  357.9 3.3 collective-permute-start.4
  361.2 6.1 %collective-permute-start.5 = (f32[1,270]{1,0:T(1,128)S(1)}, f32[1,270]{1,0:T(1,128)S(1)}, u32[]{:S(2)}, u32[]{:S(2)}) collective-permute-start(f32[1,270]{1,0:T(1,128)S(1)} %get-tuple-element.49), channel_id=1, source_target_pairs={{0,32},{32,64},{64,96},{96,128},{128,160},{160,192},{192,224},{224... | collective-permute-start | bytes 3248 | tf_op jit(solution)/shard_map/ppermute | solution.py:19
  367.4 1.9 collective-permute-start
  369.3 2.4 collective-permute-start.1
  371.7 4.9 collective-permute-done.1
  376.9 1.9 collective-permute-start.6
  378.8 7.5 %collective-permute-start.7 = (f32[1,270]{1,0:T(1,128)S(1)}, f32[1,270]{1,0:T(1,128)S(1)}, u32[]{:S(2)}, u32[]{:S(2)}) collective-permute-start(f32[1,270]{1,0:T(1,128)S(1)} %get-tuple-element.47), channel_id=1, source_target_pairs={{0,32},{32,64},{64,96},{96,128},{128,160},{160,192},{192,224},{224... | collective-permute-start | bytes 3248 | tf_op jit(solution)/shard_map/ppermute | solution.py:19
  386.4 1.9 collective-permute-start.2
  388.3 2.4 collective-permute-start.3
  390.7 4.9 collective-permute-done.3
  395.8 1.9 collective-permute-start.12
  397.8 7.5 %collective-permute-start.13 = (f32[1,270]{1,0:T(1,128)S(1)}, f32[1,270]{1,0:T(1,128)S(1)}, u32[]{:S(2)}, u32[]{:S(2)}) collective-permute-start(f32[1,270]{1,0:T(1,128)S(1)} %get-tuple-element.41), channel_id=1, source_target_pairs={{0,32},{32,64},{64,96},{96,128},{128,160},{160,192},{192,224},{224... | collective-permute-start | bytes 3248 | tf_op jit(solution)/shard_map/ppermute | solution.py:19
  405.4 1.9 collective-permute-start.8
  407.3 2.4 collective-permute-start.9
  409.7 4.9 collective-permute-done.9
  414.8 1.9 collective-permute-start.14
  416.7 7.5 %collective-permute-start.15 = (f32[1,270]{1,0:T(1,128)S(1)}, f32[1,270]{1,0:T(1,128)S(1)}, u32[]{:S(2)}, u32[]{:S(2)}) collective-permute-start(f32[1,270]{1,0:T(1,128)S(1)} %get-tuple-element.39), channel_id=1, source_target_pairs={{0,32},{32,64},{64,96},{96,128},{128,160},{160,192},{192,224},{224... | collective-permute-start | bytes 3248 | tf_op jit(solution)/shard_map/ppermute | solution.py:19
  424.3 1.9 collective-permute-start.10
  426.3 2.4 collective-permute-start.11
  428.7 4.9 collective-permute-done.11
  433.8 1.9 collective-permute-start.20
  435.7 7.5 %collective-permute-start.21 = (f32[1,270]{1,0:T(1,128)S(1)}, f32[1,270]{1,0:T(1,128)S(1)}, u32[]{:S(2)}, u32[]{:S(2)}) collective-permute-start(f32[1,270]{1,0:T(1,128)S(1)} %get-tuple-element.33), channel_id=1, source_target_pairs={{0,32},{32,64},{64,96},{96,128},{128,160},{160,192},{192,224},{224... | collective-permute-start | bytes 3248 | tf_op jit(solution)/shard_map/ppermute | solution.py:19
  443.3 1.9 collective-permute-start.16
  445.2 2.4 collective-permute-start.17
  447.7 4.9 collective-permute-done.17
  452.7 1.9 collective-permute-start.22
  454.7 7.5 %collective-permute-start.23 = (f32[1,270]{1,0:T(1,128)S(1)}, f32[1,270]{1,0:T(1,128)S(1)}, u32[]{:S(2)}, u32[]{:S(2)}) collective-permute-start(f32[1,270]{1,0:T(1,128)S(1)} %get-tuple-element.31), channel_id=1, source_target_pairs={{0,32},{32,64},{64,96},{96,128},{128,160},{160,192},{192,224},{224... | collective-permute-start | bytes 3248 | tf_op jit(solution)/shard_map/ppermute | solution.py:19
  462.3 1.9 collective-permute-start.18
  464.2 2.4 collective-permute-start.19
  466.6 4.9 collective-permute-done.19
  471.7 1.9 collective-permute-start.28
  473.6 7.5 %collective-permute-start.29 = (f32[1,270]{1,0:T(1,128)S(1)}, f32[1,270]{1,0:T(1,128)S(1)}, u32[]{:S(2)}, u32[]{:S(2)}) collective-permute-start(f32[1,270]{1,0:T(1,128)S(1)} %get-tuple-element.25), channel_id=1, source_target_pairs={{0,32},{32,64},{64,96},{96,128},{128,160},{160,192},{192,224},{224... | collective-permute-start | bytes 3248 | tf_op jit(solution)/shard_map/ppermute | solution.py:19
  481.3 1.9 collective-permute-start.24
  483.2 2.4 collective-permute-start.25
  485.6 4.9 collective-permute-done.25
  490.7 1.9 collective-permute-start.30
  492.6 7.5 %collective-permute-start.31 = (f32[1,270]{1,0:T(1,128)S(1)}, f32[1,270]{1,0:T(1,128)S(1)}, u32[]{:S(2)}, u32[]{:S(2)}) collective-permute-start(f32[1,270]{1,0:T(1,128)S(1)} %get-tuple-element.23), channel_id=1, source_target_pairs={{0,32},{32,64},{64,96},{96,128},{128,160},{160,192},{192,224},{224... | collective-permute-start | bytes 3248 | tf_op jit(solution)/shard_map/ppermute | solution.py:19
  500.3 1.9 collective-permute-start.26
  502.2 2.4 collective-permute-start.27
  504.6 4.9 collective-permute-done.27
  (75 shorter events, 4.4 us)
Async XLA Ops:
  7.2 226.8 %copy-start = (f32[4,64,2048]{2,1,0:T(8,128)S(1)}, f32[4,64,2048]{2,1,0:T(8,128)}, u32[]{:S(2)}) copy-start(f32[4,64,2048]{2,1,0:T(8,128)} %param.10) | copy-start | bytes 6291460
  7.2 226.1 %all-reduce.2.cloned.1.call-start = ((), (), s32[]{:S(2)}) async-start(), calls=%async_computation | async-start | bytes 262144 | tf_op jit(solution)/shard_map/psum | solution.py:55
  15.9 305.1 %copy-start.8 = (f32[2048]{0:T(1024)S(1)}, f32[2048]{0:T(1024)}, u32[]{:S(2)}) copy-start(f32[2048]{0:T(1024)} %param.11) | copy-start | bytes 24580
  17.9 301.3 %all-gather.3.cloned.1.call-start = ((), (), s32[]{:S(2)}) async-start(), calls=%async_computation.1 | async-start | bytes 1114112 | tf_op jit(solution)/shard_map/all_gather | solution.py:59
  235.7 121.7 %copy-start.3 = (f32[64,270]{1,0:T(8,128)S(1)}, f32[64,270]{1,0:T(8,128)}, u32[]{:S(2)}) copy-start(f32[64,270]{1,0:T(8,128)} %param.7) | copy-start | bytes 207364
  319.2 57.5 %copy-start.1 = (s32[64,270]{1,0:T(8,128)S(1)}, s32[64,270]{1,0:T(8,128)}, u32[]{:S(2)}) copy-start(s32[64,270]{1,0:T(8,128)} %param.13) | copy-start | bytes 207364
  319.2 57.5 %copy-start.6 = (f32[64,270]{1,0:T(8,128)S(1)}, f32[64,270]{1,0:T(8,128)}, u32[]{:S(2)}) copy-start(f32[64,270]{1,0:T(8,128)} %param.8) | copy-start | bytes 207364
  319.2 57.5 %copy-start.7 = (f32[64,270]{1,0:T(8,128)S(1)}, f32[64,270]{1,0:T(8,128)}, u32[]{:S(2)}) copy-start(f32[64,270]{1,0:T(8,128)} %param.9) | copy-start | bytes 207364
  357.8 113.7 %copy-start.2 = (f32[64,270]{1,0:T(8,128)}, f32[64,270]{1,0:T(8,128)S(1)}, u32[]{:S(2)}) copy-start(f32[64,270]{1,0:T(8,128)S(1)} %get-tuple-element.53) | copy-start | bytes 207364
  357.9 18.8 %collective-permute-start.4 = (f32[1,270]{1,0:T(1,128)S(1)}, f32[1,270]{1,0:T(1,128)S(1)}, u32[]{:S(2)}, u32[]{:S(2)}) collective-permute-start(f32[1,270]{1,0:T(1,128)S(1)} %get-tuple-element.48), channel_id=1, source_target_pairs={{32,0},{64,32},{96,64},{128,96},{160,128},{192,160},{224,192},{256... | collective-permute-start | bytes 3248 | tf_op jit(solution)/shard_map/ppermute | solution.py:22
  361.2 15.5 %collective-permute-start.5 = (f32[1,270]{1,0:T(1,128)S(1)}, f32[1,270]{1,0:T(1,128)S(1)}, u32[]{:S(2)}, u32[]{:S(2)}) collective-permute-start(f32[1,270]{1,0:T(1,128)S(1)} %get-tuple-element.49), channel_id=1, source_target_pairs={{0,32},{32,64},{64,96},{96,128},{128,160},{160,192},{192,224},{224... | collective-permute-start | bytes 3248 | tf_op jit(solution)/shard_map/ppermute | solution.py:19
  367.4 4.3 collective-permute-start
  369.3 7.3 %collective-permute-start.1 = (f32[64,1]{1,0:T(8,128)S(1)}, f32[64,1]{1,0:T(8,128)S(1)}, u32[]{:S(2)}, u32[]{:S(2)}) collective-permute-start(f32[64,1]{1,0:T(8,128)S(1)} %get-tuple-element.45), channel_id=1, source_target_pairs={{0,1},{1,2},{2,3},{3,4},{4,5},{5,6},{6,7},{7,8},{8,9},{9,10},{10,1... | collective-permute-start | bytes 776 | tf_op jit(solution)/shard_map/ppermute | solution.py:19
  376.9 18.8 %collective-permute-start.6 = (f32[1,270]{1,0:T(1,128)S(1)}, f32[1,270]{1,0:T(1,128)S(1)}, u32[]{:S(2)}, u32[]{:S(2)}) collective-permute-start(f32[1,270]{1,0:T(1,128)S(1)} %get-tuple-element.46), channel_id=1, source_target_pairs={{32,0},{64,32},{96,64},{128,96},{160,128},{192,160},{224,192},{256... | collective-permute-start | bytes 3248 | tf_op jit(solution)/shard_map/ppermute | solution.py:22
  378.8 16.9 %collective-permute-start.7 = (f32[1,270]{1,0:T(1,128)S(1)}, f32[1,270]{1,0:T(1,128)S(1)}, u32[]{:S(2)}, u32[]{:S(2)}) collective-permute-start(f32[1,270]{1,0:T(1,128)S(1)} %get-tuple-element.47), channel_id=1, source_target_pairs={{0,32},{32,64},{64,96},{96,128},{128,160},{160,192},{192,224},{224... | collective-permute-start | bytes 3248 | tf_op jit(solution)/shard_map/ppermute | solution.py:19
  386.4 4.3 collective-permute-start.2
  388.3 7.3 %collective-permute-start.3 = (f32[64,1]{1,0:T(8,128)S(1)}, f32[64,1]{1,0:T(8,128)S(1)}, u32[]{:S(2)}, u32[]{:S(2)}) collective-permute-start(f32[64,1]{1,0:T(8,128)S(1)} %get-tuple-element.43), channel_id=1, source_target_pairs={{0,1},{1,2},{2,3},{3,4},{4,5},{5,6},{6,7},{7,8},{8,9},{9,10},{10,1... | collective-permute-start | bytes 776 | tf_op jit(solution)/shard_map/ppermute | solution.py:19
  395.8 18.8 %collective-permute-start.12 = (f32[1,270]{1,0:T(1,128)S(1)}, f32[1,270]{1,0:T(1,128)S(1)}, u32[]{:S(2)}, u32[]{:S(2)}) collective-permute-start(f32[1,270]{1,0:T(1,128)S(1)} %get-tuple-element.40), channel_id=1, source_target_pairs={{32,0},{64,32},{96,64},{128,96},{160,128},{192,160},{224,192},{256... | collective-permute-start | bytes 3248 | tf_op jit(solution)/shard_map/ppermute | solution.py:22
  397.8 16.9 %collective-permute-start.13 = (f32[1,270]{1,0:T(1,128)S(1)}, f32[1,270]{1,0:T(1,128)S(1)}, u32[]{:S(2)}, u32[]{:S(2)}) collective-permute-start(f32[1,270]{1,0:T(1,128)S(1)} %get-tuple-element.41), channel_id=1, source_target_pairs={{0,32},{32,64},{64,96},{96,128},{128,160},{160,192},{192,224},{224... | collective-permute-start | bytes 3248 | tf_op jit(solution)/shard_map/ppermute | solution.py:19
  405.4 4.3 collective-permute-start.8
  407.3 7.3 %collective-permute-start.9 = (f32[64,1]{1,0:T(8,128)S(1)}, f32[64,1]{1,0:T(8,128)S(1)}, u32[]{:S(2)}, u32[]{:S(2)}) collective-permute-start(f32[64,1]{1,0:T(8,128)S(1)} %get-tuple-element.37), channel_id=1, source_target_pairs={{0,1},{1,2},{2,3},{3,4},{4,5},{5,6},{6,7},{7,8},{8,9},{9,10},{10,1... | collective-permute-start | bytes 776 | tf_op jit(solution)/shard_map/ppermute | solution.py:19
  414.8 18.8 %collective-permute-start.14 = (f32[1,270]{1,0:T(1,128)S(1)}, f32[1,270]{1,0:T(1,128)S(1)}, u32[]{:S(2)}, u32[]{:S(2)}) collective-permute-start(f32[1,270]{1,0:T(1,128)S(1)} %get-tuple-element.38), channel_id=1, source_target_pairs={{32,0},{64,32},{96,64},{128,96},{160,128},{192,160},{224,192},{256... | collective-permute-start | bytes 3248 | tf_op jit(solution)/shard_map/ppermute | solution.py:22
  416.7 16.9 %collective-permute-start.15 = (f32[1,270]{1,0:T(1,128)S(1)}, f32[1,270]{1,0:T(1,128)S(1)}, u32[]{:S(2)}, u32[]{:S(2)}) collective-permute-start(f32[1,270]{1,0:T(1,128)S(1)} %get-tuple-element.39), channel_id=1, source_target_pairs={{0,32},{32,64},{64,96},{96,128},{128,160},{160,192},{192,224},{224... | collective-permute-start | bytes 3248 | tf_op jit(solution)/shard_map/ppermute | solution.py:19
  424.3 4.3 collective-permute-start.10
  426.3 7.3 %collective-permute-start.11 = (f32[64,1]{1,0:T(8,128)S(1)}, f32[64,1]{1,0:T(8,128)S(1)}, u32[]{:S(2)}, u32[]{:S(2)}) collective-permute-start(f32[64,1]{1,0:T(8,128)S(1)} %get-tuple-element.35), channel_id=1, source_target_pairs={{0,1},{1,2},{2,3},{3,4},{4,5},{5,6},{6,7},{7,8},{8,9},{9,10},{10,1... | collective-permute-start | bytes 776 | tf_op jit(solution)/shard_map/ppermute | solution.py:19
  433.8 18.8 %collective-permute-start.20 = (f32[1,270]{1,0:T(1,128)S(1)}, f32[1,270]{1,0:T(1,128)S(1)}, u32[]{:S(2)}, u32[]{:S(2)}) collective-permute-start(f32[1,270]{1,0:T(1,128)S(1)} %get-tuple-element.32), channel_id=1, source_target_pairs={{32,0},{64,32},{96,64},{128,96},{160,128},{192,160},{224,192},{256... | collective-permute-start | bytes 3248 | tf_op jit(solution)/shard_map/ppermute | solution.py:22
  435.7 16.9 %collective-permute-start.21 = (f32[1,270]{1,0:T(1,128)S(1)}, f32[1,270]{1,0:T(1,128)S(1)}, u32[]{:S(2)}, u32[]{:S(2)}) collective-permute-start(f32[1,270]{1,0:T(1,128)S(1)} %get-tuple-element.33), channel_id=1, source_target_pairs={{0,32},{32,64},{64,96},{96,128},{128,160},{160,192},{192,224},{224... | collective-permute-start | bytes 3248 | tf_op jit(solution)/shard_map/ppermute | solution.py:19
  443.3 4.3 collective-permute-start.16
  445.2 7.3 %collective-permute-start.17 = (f32[64,1]{1,0:T(8,128)S(1)}, f32[64,1]{1,0:T(8,128)S(1)}, u32[]{:S(2)}, u32[]{:S(2)}) collective-permute-start(f32[64,1]{1,0:T(8,128)S(1)} %get-tuple-element.29), channel_id=1, source_target_pairs={{0,1},{1,2},{2,3},{3,4},{4,5},{5,6},{6,7},{7,8},{8,9},{9,10},{10,1... | collective-permute-start | bytes 776 | tf_op jit(solution)/shard_map/ppermute | solution.py:19
  452.7 18.8 %collective-permute-start.22 = (f32[1,270]{1,0:T(1,128)S(1)}, f32[1,270]{1,0:T(1,128)S(1)}, u32[]{:S(2)}, u32[]{:S(2)}) collective-permute-start(f32[1,270]{1,0:T(1,128)S(1)} %get-tuple-element.30), channel_id=1, source_target_pairs={{32,0},{64,32},{96,64},{128,96},{160,128},{192,160},{224,192},{256... | collective-permute-start | bytes 3248 | tf_op jit(solution)/shard_map/ppermute | solution.py:22
  454.7 16.9 %collective-permute-start.23 = (f32[1,270]{1,0:T(1,128)S(1)}, f32[1,270]{1,0:T(1,128)S(1)}, u32[]{:S(2)}, u32[]{:S(2)}) collective-permute-start(f32[1,270]{1,0:T(1,128)S(1)} %get-tuple-element.31), channel_id=1, source_target_pairs={{0,32},{32,64},{64,96},{96,128},{128,160},{160,192},{192,224},{224... | collective-permute-start | bytes 3248 | tf_op jit(solution)/shard_map/ppermute | solution.py:19
  462.3 4.3 collective-permute-start.18
  464.2 7.3 %collective-permute-start.19 = (f32[64,1]{1,0:T(8,128)S(1)}, f32[64,1]{1,0:T(8,128)S(1)}, u32[]{:S(2)}, u32[]{:S(2)}) collective-permute-start(f32[64,1]{1,0:T(8,128)S(1)} %get-tuple-element.27), channel_id=1, source_target_pairs={{0,1},{1,2},{2,3},{3,4},{4,5},{5,6},{6,7},{7,8},{8,9},{9,10},{10,1... | collective-permute-start | bytes 776 | tf_op jit(solution)/shard_map/ppermute | solution.py:19
  471.7 18.8 %collective-permute-start.28 = (f32[1,270]{1,0:T(1,128)S(1)}, f32[1,270]{1,0:T(1,128)S(1)}, u32[]{:S(2)}, u32[]{:S(2)}) collective-permute-start(f32[1,270]{1,0:T(1,128)S(1)} %get-tuple-element.24), channel_id=1, source_target_pairs={{32,0},{64,32},{96,64},{128,96},{160,128},{192,160},{224,192},{256... | collective-permute-start | bytes 3248 | tf_op jit(solution)/shard_map/ppermute | solution.py:22
  473.6 16.9 %collective-permute-start.29 = (f32[1,270]{1,0:T(1,128)S(1)}, f32[1,270]{1,0:T(1,128)S(1)}, u32[]{:S(2)}, u32[]{:S(2)}) collective-permute-start(f32[1,270]{1,0:T(1,128)S(1)} %get-tuple-element.25), channel_id=1, source_target_pairs={{0,32},{32,64},{64,96},{96,128},{128,160},{160,192},{192,224},{224... | collective-permute-start | bytes 3248 | tf_op jit(solution)/shard_map/ppermute | solution.py:19
  481.3 4.3 collective-permute-start.24
  483.2 7.3 %collective-permute-start.25 = (f32[64,1]{1,0:T(8,128)S(1)}, f32[64,1]{1,0:T(8,128)S(1)}, u32[]{:S(2)}, u32[]{:S(2)}) collective-permute-start(f32[64,1]{1,0:T(8,128)S(1)} %get-tuple-element.21), channel_id=1, source_target_pairs={{0,1},{1,2},{2,3},{3,4},{4,5},{5,6},{6,7},{7,8},{8,9},{9,10},{10,1... | collective-permute-start | bytes 776 | tf_op jit(solution)/shard_map/ppermute | solution.py:19
  490.7 19.6 %copy-start.4 = (f32[64,270]{1,0:T(8,128)}, f32[64,270]{1,0:T(8,128)S(1)}, u32[]{:S(2)}) copy-start(f32[64,270]{1,0:T(8,128)S(1)} %get-tuple-element.10) | copy-start | bytes 207364
  490.7 19.6 %copy-start.5 = (f32[64,270]{1,0:T(8,128)}, f32[64,270]{1,0:T(8,128)S(1)}, u32[]{:S(2)}) copy-start(f32[64,270]{1,0:T(8,128)S(1)} %get-tuple-element.11) | copy-start | bytes 207364
  490.7 18.8 %collective-permute-start.30 = (f32[1,270]{1,0:T(1,128)S(1)}, f32[1,270]{1,0:T(1,128)S(1)}, u32[]{:S(2)}, u32[]{:S(2)}) collective-permute-start(f32[1,270]{1,0:T(1,128)S(1)} %get-tuple-element.22), channel_id=1, source_target_pairs={{32,0},{64,32},{96,64},{128,96},{160,128},{192,160},{224,192},{256... | collective-permute-start | bytes 3248 | tf_op jit(solution)/shard_map/ppermute | solution.py:22
  492.6 16.9 %collective-permute-start.31 = (f32[1,270]{1,0:T(1,128)S(1)}, f32[1,270]{1,0:T(1,128)S(1)}, u32[]{:S(2)}, u32[]{:S(2)}) collective-permute-start(f32[1,270]{1,0:T(1,128)S(1)} %get-tuple-element.23), channel_id=1, source_target_pairs={{0,32},{32,64},{64,96},{96,128},{128,160},{160,192},{192,224},{224... | collective-permute-start | bytes 3248 | tf_op jit(solution)/shard_map/ppermute | solution.py:19
  500.3 4.3 collective-permute-start.26
  502.2 7.3 %collective-permute-start.27 = (f32[64,1]{1,0:T(8,128)S(1)}, f32[64,1]{1,0:T(8,128)S(1)}, u32[]{:S(2)}, u32[]{:S(2)}) collective-permute-start(f32[64,1]{1,0:T(8,128)S(1)} %get-tuple-element.19), channel_id=1, source_target_pairs={{0,1},{1,2},{2,3},{3,4},{4,5},{5,6},{6,7},{7,8},{8,9},{9,10},{10,1... | collective-permute-start | bytes 776 | tf_op jit(solution)/shard_map/ppermute | solution.py:19
Sparse Core Ops, SparseCore 0:
  18.0 215.1 all-reduce.1
  237.0 82.1 all-gather.2
